TPU v7x, 32 devices: a whole 2x2x4 slice. The times are simulated.
32 devices in a mesh: dom: 16 (over z, x, core), band: 2 (over y).
Axes of the slice: x: 2, y: 2, z: 4, core: 2. Of those that a mesh axis runs over, the one named last changes fastest.
Arguments:
- wavefun: float32 [13824, 512], P('dom', 'band')
- cell_ops: float32 [64, 343, 343], P('dom'), as said below
- cell_map: int32 [64, 343], P('dom'), may hold values from 0 to 1007, as said below
- face_list: int32 [2304], P('dom'), may hold values from 0 to 863, as said below
Outputs:
- ortho_bands: float32 [13824, 512], P('dom', 'band')
Inputs may be any that keep to these rules, and one draw needn't show every extreme that they name: `cell_map`: each row lists the 343 distinct local numbers of a cell's nodes; a number below 864 is a node of the cell's own domain, 864 + j stands for the j-th lower face node of the next domain (periodic over domains); every node of a domain belongs to some cell of that domain. `face_list`: the 144 entries of each domain are distinct node numbers of that domain. `cell_ops`: each cell's matrix is symmetric.
All inputs are finite; a program needn't handle non-finite values.
Results may differ from a plain program's by a relative error of at most 0.0001.
Values sent between devices are 32-bit elements; how exact they have to be, the bound alone decides.
A program may use at most 64 MiB of HBM per device.

v0:
```python
import functools
import types

import jax
import jax.numpy as jnp
from jax import lax
from jax.experimental import pallas as pl
from jax.experimental.pallas import tpu as pltpu
from jax.sharding import PartitionSpec as P

DEGREE = 2


cheb_centre = 1.0
cheb_half = 1.6

f32 = jnp.float32
bf16 = jnp.bfloat16
MESH = pl.DeviceIdType.MESH


def round_up(value, step):
    return (value + step - 1) // step * step


def halves(value):
    high = value.astype(bf16)
    low = (value - high.astype(f32)).astype(bf16)
    return high, low


def dot(left, right):
    return jnp.dot(left, right, preferred_element_type=f32)


def dot_tn(left, right):
    return lax.dot_general(left, right, (((0,), (0,)), ((), ())), preferred_element_type=f32)


def dot_nt(left, right):
    return lax.dot_general(left, right, (((1,), (1,)), ((), ())), preferred_element_type=f32)


class Sizes:
    def __init__(self, n_dom, n_band, own, width, cells, nodes, face):
        self.n_dom, self.n_band = n_dom, n_band
        self.own, self.width = own, width
        self.cells, self.nodes, self.face = cells, nodes, face
        self.own_pad = round_up(own, 128)
        self.face_pad = round_up(face, 128)
        self.rows = round_up(nodes, 16)
        self.lanes = round_up(nodes, 128)
        self.blocks = 2 if width % 256 == 0 else 1
        self.block = width // self.blocks
        self.half_pad = round_up(own // 2, 128)
        self.chips = n_dom // 2
        self.chunk = width // n_dom
        self.packet = self.chunk + 8
        self.gram = (
            n_band == 2
            and n_dom % 2 == 0
            and n_dom > 2
            and width % (8 * n_dom) == 0
            and width % 128 == 0
            and own % 32 == 0
        )


def start_all(copies):
    for copy in copies:
        copy.start()


def wait_all(copies):
    for copy in copies:
        copy.wait()


def filter_steps(s, ready, done, wave_ref, ops_ref, map_ref, face_ref, result_ref, w):
    me = lax.axis_index("dom")
    right = lax.rem(me + 1, s.n_dom)
    left = lax.rem(me + s.n_dom - 1, s.n_dom)
    C, R, L, W = s.cells, s.rows, s.lanes, s.block

    def split_store(ref, first, value):
        high, low = halves(value)
        ref[pl.ds(first, value.shape[0]), pl.ds(0, W)] = high
        ref[pl.ds(first, value.shape[0]), pl.ds(W, W)] = low

    def merged(wide):
        return wide[:, :W] + wide[:, W:]

    ops_copy = pltpu.make_async_copy(ops_ref, w.ops, w.ops_sem)
    ops_copy.start()

    w.index[...] = jnp.full(w.index.shape, -1.0, f32)
    w.index[pl.ds(0, C), pl.ds(0, s.nodes)] = map_ref[...].astype(f32)
    w.index[pl.ds(C, 1), pl.ds(0, s.face)] = face_ref[...].astype(f32)
    columns = jnp.transpose(w.index[...])

    def one_hot(match):
        return jnp.where(match, 1.0, 0.0).astype(bf16)

    def iota(shape, axis):
        return lax.broadcasted_iota(jnp.int32, shape, axis).astype(f32)

    w.face_rows[...] = one_hot(columns[: s.face, C : C + 1] == iota((s.face, s.own_pad), 1))
    for q in range(s.blocks):
        if s.own_pad > s.own:
            w.vec[q, pl.ds(s.own, s.own_pad - s.own), :] = jnp.zeros((s.own_pad - s.own, 2 * W), bf16)
        split_store(w.vec.at[q], 0, wave_ref[:, pl.ds(q * W, W)])

    def face_copy(step, q):
        return pltpu.make_async_remote_copy(
            src_ref=w.face_send.at[step, q], dst_ref=w.face_recv.at[step, q],
            send_sem=w.face_ssem.at[step, q], recv_sem=w.face_rsem.at[step, q],
            device_id={"dom": left}, device_id_type=MESH)

    def back_copy(step, q):
        return pltpu.make_async_remote_copy(
            src_ref=w.back_send.at[step, q], dst_ref=w.back_recv.at[step, q],
            send_sem=w.back_ssem.at[step, q], recv_sem=w.back_rsem.at[step, q],
            device_id={"dom": right}, device_id_type=MESH)

    def begin(step, q):
        w.face_send[step, q] = merged(dot(w.face_rows[...], w.vec[q]))
        if step == 0 and q == 0:
            ready()
        face_copy(step, q).start()

    for q in range(s.blocks):
        begin(0, q)

    w.op_pad[...] = jnp.zeros(w.op_pad.shape, f32)
    for c in range(C):
        column = columns[:R, c : c + 1]
        w.take_own[c] = one_hot(column == iota((R, s.own_pad), 1))
        w.take_face[c] = one_hot(column - float(s.own) == iota((R, s.face_pad), 1))
        row = w.index[c : c + 1, :]
        w.put_own[:, pl.ds(c * L, L)] = one_hot(row == iota((s.own, L), 0))
        w.put_face[:, pl.ds(c * L, L)] = one_hot(row - float(s.own) == iota((s.face, L), 0))
        if c == 0:
            ops_copy.wait()
        w.op_pad[c, pl.ds(0, s.nodes), pl.ds(0, s.nodes)] = w.ops[:, c, :]
        high, low = halves(w.op_pad[c])
        w.op_high[c] = high
        w.op_low[c] = low
        if L > R:
            w.prod[pl.ds(c * L + R, L - R), :] = jnp.zeros((L - R, 2 * W), bf16)
            w.cell[c, pl.ds(R, L - R), :] = jnp.zeros((L - R, 2 * W), bf16)
    w.put_back[...] = one_hot(w.index[C : C + 1, pl.ds(0, s.face_pad)] == iota((s.own, s.face_pad), 0))
    if s.face_pad > s.face:
        for q in range(s.blocks):
            w.far[q, pl.ds(s.face, s.face_pad - s.face), :] = jnp.zeros((s.face_pad - s.face, 2 * W), bf16)

    def gather(step, q):
        for c in range(C):
            w.part[q, c] = dot(w.take_own[c], w.vec[q])

    def middle(step, q):
        face_copy(step, q).wait()
        split_store(w.far.at[q], 0, w.face_recv[step, q])
        for c in range(C):
            cell = w.part[q, c] + dot(w.take_face[c], w.far[q])
            w.cell[c, pl.ds(0, R), :] = cell.astype(bf16)
            wide = dot(w.op_high[c], w.cell[c])
            value = wide[:, :W] + wide[:, W:] + dot(w.op_low[c], w.cell[c, :, pl.ds(0, W)])
            split_store(w.prod, c * L, value)
        w.back_send[step, q] = merged(dot(w.put_face[...], w.prod[...]))
        back_copy(step, q).start()
        w.applied[q] = merged(dot(w.put_own[...], w.prod[...]))

    def finish(step, q):
        back_copy(step, q).wait()
        split_store(w.far.at[q], 0, w.back_recv[step, q])
        applied = w.applied[q] + merged(dot(w.put_back[...], w.far[q]))
        columns = pl.ds(q * W, W)
        if step == 0:
            current = wave_ref[:, columns]
            following = (applied - cheb_centre * current) / cheb_half
        else:
            current = w.latest[:, columns]
            earlier = wave_ref[:, columns] if step == 1 else w.older[:, columns]
            following = 2.0 * (applied - cheb_centre * current) / cheb_half - earlier
        if step == DEGREE - 1:
            result_ref[:, columns] = following
            done(q)
        else:
            if step > 0:
                w.older[:, columns] = current
            w.latest[:, columns] = following
            split_store(w.vec.at[q], 0, following)
            begin(step + 1, q)

    gather(0, 0)
    for step in range(DEGREE):
        last = step == DEGREE - 1
        middle(step, 0)
        if s.blocks > 1:
            gather(step, 1)
        finish(step, 0)
        if s.blocks > 1:
            middle(step, 1)
        if not last:
            gather(step + 1, 0)
        if s.blocks > 1:
            finish(step, 1)


def band_copy(s, band_ref, w, turn, first, q):
    half = s.own // 2
    rows = pl.ds(pl.multiple_of(first * half, 8), half)
    columns = pl.ds(q * s.block, s.block)
    return pltpu.make_async_remote_copy(
        src_ref=band_ref.at[rows, columns], dst_ref=w.far_band.at[rows, columns],
        send_sem=w.band_ssem.at[turn, q], recv_sem=w.band_rsem.at[turn, q],
        device_id={"band": 1 - lax.axis_index("band")}, device_id_type=MESH)


def gram_steps(s, band_ref, out_ref, w):
    me = lax.axis_index("dom")
    band = lax.axis_index("band")
    other = 1 - band
    chip, core = me // 2, lax.rem(me, 2)
    partner = chip * 2 + (1 - core)
    W, half, n, chunk = s.width, s.own // 2, s.chips, s.chunk

    def core_copy(m):
        return pltpu.make_async_remote_copy(
            src_ref=w.sums.at[m, 1 - core], dst_ref=w.core_recv.at[m],
            send_sem=w.core_ssem.at[m], recv_sem=w.core_rsem.at[m],
            device_id={"dom": partner}, device_id_type=MESH)

    def scatter_copies(m):
        copies = []
        for j in range(1, n):
            target = lax.rem(chip + j, n)
            copies.append(pltpu.make_async_remote_copy(
                src_ref=w.pair.at[m, target], dst_ref=w.scat_recv.at[m, j - 1],
                send_sem=w.scat_ssem.at[m, j - 1], recv_sem=w.scat_rsem.at[m, j - 1],
                device_id={"dom": target * 2 + core}, device_id_type=MESH))
        return copies

    def gather_copies(m):
        copies = []
        for j in range(1, n):
            target = lax.rem(chip + j, n)
            copies.append(pltpu.make_async_remote_copy(
                src_ref=w.full.at[m, core, chip], dst_ref=w.full.at[m, core, chip],
                send_sem=w.gath_ssem.at[m, j - 1], recv_sem=w.gath_rsem.at[m, j - 1],
                device_id={"dom": target * 2 + core}, device_id_type=MESH))
        return copies

    def swap_copy(m):
        return pltpu.make_async_remote_copy(
            src_ref=w.full.at[m, core], dst_ref=w.full.at[m, core],
            send_sem=w.swap_ssem.at[m], recv_sem=w.swap_rsem.at[m],
            device_id={"dom": partner}, device_id_type=MESH)

    def cross_copy():
        return pltpu.make_async_remote_copy(
            src_ref=w.cross_send, dst_ref=w.cross_recv,
            send_sem=w.cross_ssem, recv_sem=w.cross_rsem,
            device_id={"band": other}, device_id_type=MESH)

    def put_sums(m, value):
        w.sums[m] = value.reshape(2, W // 2, W)

    def pair_up(m):
        core_copy(m).wait()
        total = w.sums[m, core] + w.core_recv[m]
        w.pair[m] = total.reshape(n, chunk, W)

    def own_total(m):
        wait_all(scatter_copies(m))
        total = w.pair[m, chip]
        for j in range(n - 1):
            total = total + w.scat_recv[m, j]
        return total

    high, low = halves(band_ref[...])
    def fill(ref, value):
        count, size = value.shape[0], ref.shape[0]
        ref[pl.ds(0, count), :] = value
        if size > count:
            ref[pl.ds(count, size - count), :] = jnp.zeros((size - count, W), bf16)

    fill(w.near_high, high)
    fill(w.near_low, low)
    turned_high, turned_low = halves(jnp.transpose(w.bands[...]))
    put_sums(0, dot(turned_high, w.near_high[...])
             + dot(turned_high, w.near_low[...])
             + dot(turned_low, w.near_high[...]))
    core_copy(0).start()
    pair_up(0)
    start_all(scatter_copies(0))
    same = own_total(0)
    w.full[0, core, chip, pl.ds(0, chunk), :] = same
    squares = (same * same).reshape(chunk // 8, 8, W).sum(0)
    w.full[0, core, chip, pl.ds(chunk, 8), :] = squares
    start_all(gather_copies(0))

    for q in range(s.blocks):
        band_copy(s, band_ref, w, 0, other, q).wait_send()
        band_copy(s, band_ref, w, 0, band, q).wait_recv()
    for q in range(s.blocks):
        band_copy(s, band_ref, w, 1, band, q).start()
    rows = pl.ds(pl.multiple_of(band * half, 16), half)
    far_high, far_low = halves(w.far_band[rows, :])
    near_high, near_low = w.near_high[rows, :], w.near_low[rows, :]
    first = band == 0

    def pick(a, b):
        return jnp.where(first, a, b)

    fill(w.left_high, pick(far_high, near_high))
    fill(w.left_low, pick(far_low, near_low))
    fill(w.right_high, pick(near_high, far_high))
    fill(w.right_low, pick(near_low, far_low))
    put_sums(1, dot_tn(w.left_high[...], w.right_high[...])
             + dot_tn(w.left_high[...], w.right_low[...])
             + dot_tn(w.left_low[...], w.right_high[...]))
    core_copy(1).start()
    pair_up(1)
    start_all(scatter_copies(1))

    wait_all(gather_copies(0))
    swap_copy(0).start()
    cross = own_total(1)
    w.cross_send[pl.ds(0, chunk), :] = cross
    w.cross_send[pl.ds(chunk, 8), :] = squares
    cross_copy().start()
    cross_copy().wait()
    cross = pick(cross, w.cross_recv[pl.ds(0, chunk), :]) + pick(w.cross_recv[pl.ds(0, chunk), :], cross)
    w.full[1, core, chip, pl.ds(0, chunk), :] = cross
    w.full[1, core, chip, pl.ds(chunk, 8), :] = (
        2.0 * (cross * cross).reshape(chunk // 8, 8, W).sum(0) + w.cross_recv[pl.ds(chunk, 8), :])
    start_all(gather_copies(1))
    swap_copy(0).wait()
    near_block = w.full[0, :, :, pl.ds(0, chunk), :].reshape(W, W)
    block_high, block_low = halves(near_block)
    w.block_high[0] = block_high
    w.block_low[0] = block_low
    near_high, near_low = w.near_high[pl.ds(0, s.own), :], w.near_low[pl.ds(0, s.own), :]
    near_wide = dot(near_high, w.block_high[0]) + dot(near_high, w.block_low[0])
    w.near_prod[...] = near_wide + dot(near_low, w.block_high[0])
    for q in range(s.blocks):
        band_copy(s, band_ref, w, 1, band, q).wait_send()
        band_copy(s, band_ref, w, 1, other, q).wait_recv()
    high, low = halves(w.far_band[...])
    w.far_high[...] = high
    w.far_low[...] = low
    wait_all(gather_copies(1))
    swap_copy(1).start()
    swap_copy(1).wait()
    total = jnp.sum(w.full[:, :, :, pl.ds(chunk, 8), :])
    norm = jnp.sqrt(jnp.full((1, W), total, f32) + 1e-06)
    far_block = w.full[1, :, :, pl.ds(0, chunk), :].reshape(W, W)
    far_block = pick(far_block, jnp.transpose(far_block))
    block_high, block_low = halves(far_block)
    w.block_high[1] = block_high
    w.block_low[1] = block_low
    wide = dot(w.far_high[...], w.block_high[1]) + dot(w.far_high[...], w.block_low[1])
    wide = wide + dot(w.far_low[...], w.block_high[1]) + w.near_prod[...]
    out_ref[...] = 1.5 * band_ref[...] - wide * (0.5 / norm)


def kernel(s, names, wave_ref, ops_ref, map_ref, face_ref, out_ref, *scratch):
    w = types.SimpleNamespace(**dict(zip(names, scratch)))
    me = lax.axis_index("dom")
    barrier = pltpu.get_barrier_semaphore()
    greeted = [{"dom": lax.rem(me + 1, s.n_dom)}, {"dom": lax.rem(me + s.n_dom - 1, s.n_dom)}]
    if s.gram:
        chip, core = me // 2, lax.rem(me, 2)
        greeted.append({"dom": chip * 2 + (1 - core)})
        greeted.append({"band": 1 - lax.axis_index("band")})
        for j in range(1, s.chips):
            greeted.append({"dom": lax.rem(chip + j, s.chips) * 2 + core})
    for device in greeted:
        pl.semaphore_signal(barrier, inc=1, device_id=device, device_id_type=MESH)

    def ready():
        pl.semaphore_wait(barrier, len(greeted))

    if s.gram:
        if s.own_pad > s.own:
            w.bands[pl.ds(s.own, s.own_pad - s.own), :] = jnp.zeros((s.own_pad - s.own, s.width), f32)
        owned = w.bands.at[pl.ds(0, s.own), :]

        def send(q):
            band_copy(s, owned, w, 0, 1 - lax.axis_index("band"), q).start()

        filter_steps(s, ready, send, wave_ref, ops_ref, map_ref, face_ref, owned, w)
        gram_steps(s, owned, out_ref, w)
    else:
        filter_steps(s, ready, lambda q: None, wave_ref, ops_ref, map_ref, face_ref, out_ref, w)


def scratch_of(s):
    C, R, L, W, n, chunk = s.cells, s.rows, s.lanes, s.width, s.chips, s.chunk
    V, dma = pltpu.VMEM, pltpu.SemaphoreType.DMA
    scratch = dict(
        index=V((128, max(L, s.face_pad)), f32),
        face_rows=V((s.face, s.own_pad), bf16),
        vec=V((s.blocks, s.own_pad, 2 * s.block), bf16),
        take_own=V((C, R, s.own_pad), bf16),
        take_face=V((C, R, s.face_pad), bf16),
        put_own=V((s.own, C * L), bf16),
        put_face=V((s.face, C * L), bf16),
        put_back=V((s.own, s.face_pad), bf16),
        ops=V((s.nodes, C, s.nodes), f32),
        ops_sem=dma,
        op_pad=V((C, R, L), f32),
        op_high=V((C, R, L), bf16),
        op_low=V((C, R, L), bf16),
        part=V((s.blocks, C, R, 2 * s.block), f32),
        applied=V((s.blocks, s.own, s.block), f32),
        cell=V((C, L, 2 * s.block), bf16),
        prod=V((C * L, 2 * s.block), bf16),
        far=V((s.blocks, s.face_pad, 2 * s.block), bf16),
        latest=V((s.own, W), f32),
        older=V((s.own, W) if DEGREE > 2 else (8, 128), f32),
        face_send=V((DEGREE, s.blocks, s.face, s.block), f32),
        face_recv=V((DEGREE, s.blocks, s.face, s.block), f32),
        back_send=V((DEGREE, s.blocks, s.face, s.block), f32),
        back_recv=V((DEGREE, s.blocks, s.face, s.block), f32),
        face_ssem=dma((DEGREE, s.blocks)),
        face_rsem=dma((DEGREE, s.blocks)),
        back_ssem=dma((DEGREE, s.blocks)),
        back_rsem=dma((DEGREE, s.blocks)),
    )
    if s.gram:
        scratch |= dict(
            bands=V((s.own_pad, W), f32),
            far_band=V((s.own, W), f32),
            near_high=V((s.own_pad, W), bf16),
            near_low=V((s.own_pad, W), bf16),
            left_high=V((s.half_pad, W), bf16),
            left_low=V((s.half_pad, W), bf16),
            right_high=V((s.half_pad, W), bf16),
            right_low=V((s.half_pad, W), bf16),
            far_high=V((s.own, W), bf16),
            far_low=V((s.own, W), bf16),
            near_prod=V((s.own, W), f32),
            block_high=V((2, W, W), bf16),
            block_low=V((2, W, W), bf16),
            sums=V((2, 2, W // 2, W), f32),
            core_recv=V((2, W // 2, W), f32),
            pair=V((2, n, chunk, W), f32),
            scat_recv=V((2, n - 1, chunk, W), f32),
            full=V((2, 2, n, s.packet, W), f32),
            cross_send=V((s.packet, W), f32),
            cross_recv=V((s.packet, W), f32),
            cross_ssem=dma,
            cross_rsem=dma,
            band_ssem=dma((2, s.blocks)),
            band_rsem=dma((2, s.blocks)),
            core_ssem=dma((2,)),
            core_rsem=dma((2,)),
            swap_ssem=dma((2,)),
            swap_rsem=dma((2,)),
            scat_ssem=dma((2, n - 1)),
            scat_rsem=dma((2, n - 1)),
            gath_ssem=dma((2, n - 1)),
            gath_rsem=dma((2, n - 1)),
        )
    return scratch


def on_device(wavefun, cell_ops, cell_map, face_list):
    s = Sizes(lax.axis_size("dom"), lax.axis_size("band"), wavefun.shape[0], wavefun.shape[1],
              cell_map.shape[0], cell_map.shape[1], face_list.shape[0])
    scratch = scratch_of(s)
    latest = pl.pallas_call(
        functools.partial(kernel, s, list(scratch)),
        out_shape=jax.ShapeDtypeStruct(wavefun.shape, f32),
        in_specs=[pl.BlockSpec(memory_space=space) for space in (pltpu.VMEM, pl.ANY, pltpu.VMEM, pltpu.VMEM)],
        out_specs=pl.BlockSpec(memory_space=pltpu.VMEM),
        scratch_shapes=list(scratch.values()),
        compiler_params=pltpu.CompilerParams(
            collective_id=0, has_side_effects=True, vmem_limit_bytes=60 * 1024 * 1024),
        name="filtered_bands",
    )(wavefun, jnp.swapaxes(cell_ops, 0, 1), cell_map, face_list.reshape(1, -1))
    if s.gram:
        return latest
    full_bands = lax.all_gather(latest, "band", axis=1, tiled=True)
    partial_value = jnp.einsum("nb,nc->bc", full_bands, full_bands, precision=lax.Precision.HIGHEST)
    margin = lax.psum(partial_value, "dom")
    norm_value = jnp.sqrt(jnp.sum(margin * margin) + 1e-06)
    full_width = margin.shape[0]
    offset = lax.axis_index("band") * s.width
    scaled_cols = lax.dynamic_slice_in_dim(margin, offset, s.width, 1) / norm_value
    identity_cols = lax.dynamic_slice_in_dim(
        jnp.eye(full_width, dtype=jnp.float32), offset, s.width, 1
    )
    mixing = (3.0 * identity_cols - scaled_cols) / 2.0
    return jnp.dot(full_bands, mixing, precision=lax.Precision.HIGHEST)


def solution(mesh):
    return jax.shard_map(
        on_device,
        mesh=mesh,
        in_specs=(P("dom", "band"), P("dom", None, None), P("dom", None), P("dom")),
        out_specs=P("dom", "band"),
        check_vma=False,
    )
```

profile of v0, /device:TPU:0, one launch (start us, length us, event | category | flops | bytes accessed | tf_op | source)
XLA Modules:
  0.0 63.6 jit_solution(9372383481689751479)
XLA Ops:
  0.0 61.4 %filtered_bands.1 = f32[864,256]{1,0:T(8,128)} custom-call(f32[864,256]{1,0:T(8,128)} %wave_ref.1, f32[343,4,343]{2,1,0:T(4,128)} %bitcast.2, s32[4,343]{1,0:T(4,128)} %map_ref.1, s32[1,144]{1,0:T(1,128)} %bitcast.3), custom_call_target="tpu_custom_call" | custom-call | tf_op jit(solution)/shard_map/filtered_bands/pallas_call | solution.py:474
  61.4 2.1 %copy.6 = f32[864,256]{1,0:T(8,128)} copy(f32[864,256]{1,0:T(8,128)} %filtered_bands.1) | data formatting | bytes 1769472
where the time goes:
time: 63.7 us; the launch traced here: 63.6 us
  Pallas kernels  61.4 us (96%)
  local copies, waits for them, and re-layouts  2.14 us (3%)
    pallas_call x1, Pallas kernels, on_device(): pl.pallas_call(functools.partial(kernel, s, list(scratch)), out_shape=jax...  61.4 us
    unnamed x1, local copies, waits for them, and re-layouts  2.14 us

commit v1 on v0

--- a/solution.py
+++ b/solution.py
@@ -52,6 +52,8 @@
         self.lanes = round_up(nodes, 128)
         self.blocks = 2 if width % 256 == 0 else 1
         self.block = width // self.blocks
+        self.depth = round_up(own + face, 128)
+        self.base = own // 128 * 128
         self.half_pad = round_up(own // 2, 128)
         self.chips = n_dom // 2
         self.chunk = width // n_dom
@@ -81,6 +83,7 @@
     right = lax.rem(me + 1, s.n_dom)
     left = lax.rem(me + s.n_dom - 1, s.n_dom)
     C, R, L, W = s.cells, s.rows, s.lanes, s.block
+    known = s.own + s.face
 
     def split_store(ref, first, value):
         high, low = halves(value)
@@ -104,107 +107,140 @@
     def iota(shape, axis):
         return lax.broadcasted_iota(jnp.int32, shape, axis).astype(f32)
 
-    w.face_rows[...] = one_hot(columns[: s.face, C : C + 1] == iota((s.face, s.own_pad), 1))
+    faces = columns[: s.face, C : C + 1]
+    w.face_rows[...] = one_hot(faces == iota((s.face, s.own_pad), 1))
     for q in range(s.blocks):
-        if s.own_pad > s.own:
-            w.vec[q, pl.ds(s.own, s.own_pad - s.own), :] = jnp.zeros((s.own_pad - s.own, 2 * W), bf16)
+        w.vec[q, pl.ds(s.own, s.depth - s.own), :] = jnp.zeros((s.depth - s.own, 2 * W), bf16)
         split_store(w.vec.at[q], 0, wave_ref[:, pl.ds(q * W, W)])
-
-    def face_copy(step, q):
+        w.face_send[q] = merged(dot(w.face_rows[...], w.vec[q, pl.ds(0, s.own_pad), :]))
+
+    def remote(send, recv, send_sem, recv_sem, target):
         return pltpu.make_async_remote_copy(
-            src_ref=w.face_send.at[step, q], dst_ref=w.face_recv.at[step, q],
-            send_sem=w.face_ssem.at[step, q], recv_sem=w.face_rsem.at[step, q],
-            device_id={"dom": left}, device_id_type=MESH)
+            src_ref=send, dst_ref=recv, send_sem=send_sem, recv_sem=recv_sem,
+            device_id={"dom": target}, device_id_type=MESH)
+
+    def face_copy(q):
+        return remote(w.face_send.at[q], w.face_recv.at[q], w.face_ssem.at[q], w.face_rsem.at[q], left)
 
     def back_copy(step, q):
-        return pltpu.make_async_remote_copy(
-            src_ref=w.back_send.at[step, q], dst_ref=w.back_recv.at[step, q],
-            send_sem=w.back_ssem.at[step, q], recv_sem=w.back_rsem.at[step, q],
-            device_id={"dom": right}, device_id_type=MESH)
-
-    def begin(step, q):
-        w.face_send[step, q] = merged(dot(w.face_rows[...], w.vec[q]))
-        if step == 0 and q == 0:
-            ready()
-        face_copy(step, q).start()
-
-    for q in range(s.blocks):
-        begin(0, q)
-
-    w.op_pad[...] = jnp.zeros(w.op_pad.shape, f32)
-    for c in range(C):
-        column = columns[:R, c : c + 1]
-        w.take_own[c] = one_hot(column == iota((R, s.own_pad), 1))
-        w.take_face[c] = one_hot(column - float(s.own) == iota((R, s.face_pad), 1))
-        row = w.index[c : c + 1, :]
-        w.put_own[:, pl.ds(c * L, L)] = one_hot(row == iota((s.own, L), 0))
-        w.put_face[:, pl.ds(c * L, L)] = one_hot(row - float(s.own) == iota((s.face, L), 0))
-        if c == 0:
-            ops_copy.wait()
-        w.op_pad[c, pl.ds(0, s.nodes), pl.ds(0, s.nodes)] = w.ops[:, c, :]
-        high, low = halves(w.op_pad[c])
-        w.op_high[c] = high
-        w.op_low[c] = low
-        if L > R:
-            w.prod[pl.ds(c * L + R, L - R), :] = jnp.zeros((L - R, 2 * W), bf16)
-            w.cell[c, pl.ds(R, L - R), :] = jnp.zeros((L - R, 2 * W), bf16)
-    w.put_back[...] = one_hot(w.index[C : C + 1, pl.ds(0, s.face_pad)] == iota((s.own, s.face_pad), 0))
-    if s.face_pad > s.face:
+        return remote(w.back_send.at[step, q], w.back_recv.at[step, q],
+                      w.back_ssem.at[step, q], w.back_rsem.at[step, q], right)
+
+    def edge_copy(step, q):
+        return remote(w.edge_send.at[step, q], w.edge_recv.at[step, q],
+                      w.edge_ssem.at[step, q], w.edge_rsem.at[step, q], left)
+
+    def setup_take():
+        for c in range(C):
+            w.take[pl.ds(c * R, R), :] = one_hot(columns[:R, c : c + 1] == iota((R, s.depth), 1))
+
+    def setup_ops():
+        w.op_pad[...] = jnp.zeros(w.op_pad.shape, f32)
+        ops_copy.wait()
+        for c in range(C):
+            w.op_pad[c, pl.ds(0, s.nodes), pl.ds(0, s.nodes)] = w.ops[:, c, :]
+            high, low = halves(w.op_pad[c])
+            w.op_high[c] = high
+            w.op_low[c] = low
+
+    def setup_put():
+        for c in range(C):
+            row = w.index[c : c + 1, pl.ds(0, L)]
+            w.put[pl.ds(0, known), pl.ds(c * L, L)] = one_hot(row == iota((known, L), 0))
+            w.put[pl.ds(known, s.face), pl.ds(c * L, L)] = one_hot(row == faces)
+            if L > R:
+                for q in range(s.blocks):
+                    w.prod[q, pl.ds(c * L + R, L - R), :] = jnp.zeros((L - R, 2 * W), bf16)
+                w.cell[c, pl.ds(R, L - R), :] = jnp.zeros((L - R, 2 * W), bf16)
+        w.put_back[...] = one_hot(w.index[C : C + 1, pl.ds(0, s.face_pad)] == iota((s.own, s.face_pad), 0))
         for q in range(s.blocks):
-            w.far[q, pl.ds(s.face, s.face_pad - s.face), :] = jnp.zeros((s.face_pad - s.face, 2 * W), bf16)
-
-    def gather(step, q):
+            w.far[q] = jnp.zeros(w.far.shape[1:], bf16)
+            if s.face_pad > s.face:
+                w.back[q, pl.ds(s.face, s.face_pad - s.face), :] = jnp.zeros((s.face_pad - s.face, 2 * W), bf16)
+
+    def gather(q):
+        w.part[q] = dot(w.take[:, pl.ds(0, s.own_pad)], w.vec[q, pl.ds(0, s.own_pad), :])
+
+    def middle(step, q):
+        last = step == DEGREE - 1
+        if step == 0:
+            face_copy(q).wait()
+            split_store(w.far.at[q], s.own - s.base, w.face_recv[q])
         for c in range(C):
-            w.part[q, c] = dot(w.take_own[c], w.vec[q])
-
-    def middle(step, q):
-        face_copy(step, q).wait()
-        split_store(w.far.at[q], 0, w.face_recv[step, q])
+            rows = pl.ds(c * R, R)
+            if step == 0:
+                cell = w.part[q, rows, :] + dot(w.take[rows, pl.ds(s.base, s.depth - s.base)], w.far[q])
+            else:
+                cell = dot(w.take[rows, :], w.vec[q])
+            w.cell[c, pl.ds(0, R), :] = cell.astype(bf16)
         for c in range(C):
-            cell = w.part[q, c] + dot(w.take_face[c], w.far[q])
-            w.cell[c, pl.ds(0, R), :] = cell.astype(bf16)
             wide = dot(w.op_high[c], w.cell[c])
             value = wide[:, :W] + wide[:, W:] + dot(w.op_low[c], w.cell[c, :, pl.ds(0, W)])
-            split_store(w.prod, c * L, value)
-        w.back_send[step, q] = merged(dot(w.put_face[...], w.prod[...]))
+            split_store(w.prod.at[q], c * L, value)
+        count = s.face if last else 2 * s.face
+        tail = merged(dot(w.put[pl.ds(s.own, count), :], w.prod[q]))
+        w.back_send[step, q] = tail[: s.face]
         back_copy(step, q).start()
-        w.applied[q] = merged(dot(w.put_own[...], w.prod[...]))
+        if not last:
+            w.edge_send[step, q] = tail[s.face :]
+            edge_copy(step, q).start()
+
+    def scatter(q):
+        w.applied[q] = merged(dot(w.put[pl.ds(0, s.own), :], w.prod[q]))
+
+    def advance(step, applied, current, earlier):
+        if step == 0:
+            return (applied - cheb_centre * current) / cheb_half
+        return 2.0 * (applied - cheb_centre * current) / cheb_half - earlier
 
     def finish(step, q):
         back_copy(step, q).wait()
-        split_store(w.far.at[q], 0, w.back_recv[step, q])
-        applied = w.applied[q] + merged(dot(w.put_back[...], w.far[q]))
+        split_store(w.back.at[q], 0, w.back_recv[step, q])
+        applied = w.applied[q] + merged(dot(w.put_back[...], w.back[q]))
         columns = pl.ds(q * W, W)
-        if step == 0:
-            current = wave_ref[:, columns]
-            following = (applied - cheb_centre * current) / cheb_half
-        else:
-            current = w.latest[:, columns]
-            earlier = wave_ref[:, columns] if step == 1 else w.older[:, columns]
-            following = 2.0 * (applied - cheb_centre * current) / cheb_half - earlier
+
+        def stage(k):
+            return wave_ref[:, columns] if k == 0 else w.stages[k - 1, :, columns]
+
+        following = advance(step, applied, stage(step), stage(step - 1) if step else None)
         if step == DEGREE - 1:
             result_ref[:, columns] = following
             done(q)
-        else:
-            if step > 0:
-                w.older[:, columns] = current
-            w.latest[:, columns] = following
-            split_store(w.vec.at[q], 0, following)
-            begin(step + 1, q)
-
-    gather(0, 0)
-    for step in range(DEGREE):
-        last = step == DEGREE - 1
-        middle(step, 0)
-        if s.blocks > 1:
-            gather(step, 1)
-        finish(step, 0)
-        if s.blocks > 1:
-            middle(step, 1)
-        if not last:
-            gather(step + 1, 0)
-        if s.blocks > 1:
-            finish(step, 1)
+            return
+        w.stages[step, :, columns] = following
+        split_store(w.vec.at[q], 0, following)
+        edge_copy(step, q).wait()
+
+        def edge(k):
+            return w.face_recv[q] if k == 0 else w.edges[k - 1, q]
+
+        outer = advance(step, w.back_send[step, q] + w.edge_recv[step, q], edge(step), edge(step - 1) if step else None)
+        w.edges[step, q] = outer
+        split_store(w.vec.at[q], s.own, outer)
+
+    blocks = range(s.blocks)
+    setup_take()
+    setup_ops()
+    setup_put()
+    ready()
+    for q in blocks:
+        face_copy(q).start()
+    for q in blocks:
+        gather(q)
+    for q in blocks:
+        middle(0, q)
+    for q in blocks:
+        scatter(q)
+    for step in range(1, DEGREE):
+        for q in blocks:
+            finish(step - 1, q)
+            middle(step, q)
+        if step < DEGREE - 1:
+            for q in blocks:
+                scatter(q)
+    for q in blocks:
+        scatter(q)
+        finish(DEGREE - 1, q)
 
 
 def band_copy(s, band_ref, w, turn, first, q):
@@ -402,30 +438,33 @@
     scratch = dict(
         index=V((128, max(L, s.face_pad)), f32),
         face_rows=V((s.face, s.own_pad), bf16),
-        vec=V((s.blocks, s.own_pad, 2 * s.block), bf16),
-        take_own=V((C, R, s.own_pad), bf16),
-        take_face=V((C, R, s.face_pad), bf16),
-        put_own=V((s.own, C * L), bf16),
-        put_face=V((s.face, C * L), bf16),
+        vec=V((s.blocks, s.depth, 2 * s.block), bf16),
+        take=V((C * R, s.depth), bf16),
+        put=V((s.own + 2 * s.face, C * L), bf16),
         put_back=V((s.own, s.face_pad), bf16),
         ops=V((s.nodes, C, s.nodes), f32),
         ops_sem=dma,
         op_pad=V((C, R, L), f32),
         op_high=V((C, R, L), bf16),
         op_low=V((C, R, L), bf16),
-        part=V((s.blocks, C, R, 2 * s.block), f32),
+        part=V((s.blocks, C * R, 2 * s.block), f32),
         applied=V((s.blocks, s.own, s.block), f32),
         cell=V((C, L, 2 * s.block), bf16),
-        prod=V((C * L, 2 * s.block), bf16),
-        far=V((s.blocks, s.face_pad, 2 * s.block), bf16),
-        latest=V((s.own, W), f32),
-        older=V((s.own, W) if DEGREE > 2 else (8, 128), f32),
-        face_send=V((DEGREE, s.blocks, s.face, s.block), f32),
-        face_recv=V((DEGREE, s.blocks, s.face, s.block), f32),
+        prod=V((s.blocks, C * L, 2 * s.block), bf16),
+        far=V((s.blocks, s.depth - s.base, 2 * s.block), bf16),
+        back=V((s.blocks, s.face_pad, 2 * s.block), bf16),
+        stages=V((DEGREE - 1, s.own, W), f32),
+        edges=V((DEGREE - 1, s.blocks, s.face, s.block), f32),
+        face_send=V((s.blocks, s.face, s.block), f32),
+        face_recv=V((s.blocks, s.face, s.block), f32),
+        edge_send=V((DEGREE - 1, s.blocks, s.face, s.block), f32),
+        edge_recv=V((DEGREE - 1, s.blocks, s.face, s.block), f32),
         back_send=V((DEGREE, s.blocks, s.face, s.block), f32),
         back_recv=V((DEGREE, s.blocks, s.face, s.block), f32),
-        face_ssem=dma((DEGREE, s.blocks)),
-        face_rsem=dma((DEGREE, s.blocks)),
+        face_ssem=dma((s.blocks,)),
+        face_rsem=dma((s.blocks,)),
+        edge_ssem=dma((DEGREE - 1, s.blocks)),
+        edge_rsem=dma((DEGREE - 1, s.blocks)),
         back_ssem=dma((DEGREE, s.blocks)),
         back_rsem=dma((DEGREE, s.blocks)),
     )

time: 63.7 us -> 56.8 us (0.89)
  Pallas kernels: 61.4 us -> 54.5 us
    pallas_call x1, Pallas kernels: 61.4 us -> 54.5 us  [on_device(): pl.pallas_call(functools.partial(kernel, s, list(scratch)), out_shape=jax...]
where the time goes in v1:
time: 56.8 us; the launch traced here: 56.6 us
  Pallas kernels  54.5 us (96%)
  local copies, waits for them, and re-layouts  2.14 us (4%)
    pallas_call x1, Pallas kernels, on_device(): pl.pallas_call(functools.partial(kernel, s, list(scratch)), out_shape=jax...  54.5 us
    unnamed x1, local copies, waits for them, and re-layouts  2.14 us

profile of v1, /device:TPU:0, one launch (start us, length us, event | category | flops | bytes accessed | tf_op | source)
XLA Modules:
  0.0 56.6 jit_solution(18239877265355429964)
XLA Ops:
  0.0 54.5 %filtered_bands.1 = f32[864,256]{1,0:T(8,128)} custom-call(f32[864,256]{1,0:T(8,128)} %wave_ref.1, f32[343,4,343]{2,1,0:T(4,128)} %bitcast.2, s32[4,343]{1,0:T(4,128)} %map_ref.1, s32[1,144]{1,0:T(1,128)} %bitcast.3), custom_call_target="tpu_custom_call" | custom-call | tf_op jit(solution)/shard_map/filtered_bands/pallas_call | solution.py:513
  54.5 2.1 %copy.6 = f32[864,256]{1,0:T(8,128)} copy(f32[864,256]{1,0:T(8,128)} %filtered_bands.1) | data formatting | bytes 1769472

commit v2 on v1

--- a/solution.py
+++ b/solution.py
@@ -57,7 +57,6 @@
         self.half_pad = round_up(own // 2, 128)
         self.chips = n_dom // 2
         self.chunk = width // n_dom
-        self.packet = self.chunk + 8
         self.gram = (
             n_band == 2
             and n_dom % 2 == 0
@@ -78,23 +77,33 @@
         copy.wait()
 
 
-def filter_steps(s, ready, done, wave_ref, ops_ref, map_ref, face_ref, result_ref, w):
+def filter_steps(s, greet, ready, done, wave_ref, ops_ref, map_ref, face_ref, result_ref, w):
     me = lax.axis_index("dom")
     right = lax.rem(me + 1, s.n_dom)
     left = lax.rem(me + s.n_dom - 1, s.n_dom)
     C, R, L, W = s.cells, s.rows, s.lanes, s.block
     known = s.own + s.face
-
-    def split_store(ref, first, value):
+    blocks = range(s.blocks)
+
+    def span(q):
+        return pl.ds(2 * q * W, 2 * W)
+
+    def split_store(ref, first, value, q=0):
         high, low = halves(value)
-        ref[pl.ds(first, value.shape[0]), pl.ds(0, W)] = high
-        ref[pl.ds(first, value.shape[0]), pl.ds(W, W)] = low
-
-    def merged(wide):
-        return wide[:, :W] + wide[:, W:]
-
-    ops_copy = pltpu.make_async_copy(ops_ref, w.ops, w.ops_sem)
-    ops_copy.start()
+        ref[pl.ds(first, value.shape[0]), pl.ds(2 * q * W, W)] = high
+        ref[pl.ds(first, value.shape[0]), pl.ds((2 * q + 1) * W, W)] = low
+
+    def merged(wide, q=0):
+        return wide[:, 2 * q * W : (2 * q + 1) * W] + wide[:, (2 * q + 1) * W : (2 * q + 2) * W]
+
+    inputs = []
+    for k, (source, target) in enumerate(zip((map_ref, face_ref, wave_ref, ops_ref), (w.map, w.face, w.wave, w.ops))):
+        inputs.append(pltpu.make_async_copy(source, target, w.input_sem.at[k]))
+        inputs[k].start()
+    greet()
+    map_ref, face_ref, wave_ref = w.map, w.face, w.wave
+    inputs[0].wait()
+    inputs[1].wait()
 
     w.index[...] = jnp.full(w.index.shape, -1.0, f32)
     w.index[pl.ds(0, C), pl.ds(0, s.nodes)] = map_ref[...].astype(f32)
@@ -109,10 +118,13 @@
 
     faces = columns[: s.face, C : C + 1]
     w.face_rows[...] = one_hot(faces == iota((s.face, s.own_pad), 1))
-    for q in range(s.blocks):
-        w.vec[q, pl.ds(s.own, s.depth - s.own), :] = jnp.zeros((s.depth - s.own, 2 * W), bf16)
-        split_store(w.vec.at[q], 0, wave_ref[:, pl.ds(q * W, W)])
-        w.face_send[q] = merged(dot(w.face_rows[...], w.vec[q, pl.ds(0, s.own_pad), :]))
+    w.vec[pl.ds(s.own, s.depth - s.own), :] = jnp.zeros((s.depth - s.own, w.vec.shape[1]), bf16)
+    inputs[2].wait()
+    for q in blocks:
+        split_store(w.vec, 0, wave_ref[:, pl.ds(q * W, W)], q)
+    lower = dot(w.face_rows[...], w.vec[pl.ds(0, s.own_pad), :])
+    for q in blocks:
+        w.face_send[q] = merged(lower, q)
 
     def remote(send, recv, send_sem, recv_sem, target):
         return pltpu.make_async_remote_copy(
@@ -136,7 +148,7 @@
 
     def setup_ops():
         w.op_pad[...] = jnp.zeros(w.op_pad.shape, f32)
-        ops_copy.wait()
+        inputs[3].wait()
         for c in range(C):
             w.op_pad[c, pl.ds(0, s.nodes), pl.ds(0, s.nodes)] = w.ops[:, c, :]
             high, low = halves(w.op_pad[c])
@@ -149,8 +161,7 @@
             w.put[pl.ds(0, known), pl.ds(c * L, L)] = one_hot(row == iota((known, L), 0))
             w.put[pl.ds(known, s.face), pl.ds(c * L, L)] = one_hot(row == faces)
             if L > R:
-                for q in range(s.blocks):
-                    w.prod[q, pl.ds(c * L + R, L - R), :] = jnp.zeros((L - R, 2 * W), bf16)
+                w.prod[pl.ds(c * L + R, L - R), :] = jnp.zeros((L - R, w.prod.shape[1]), bf16)
                 w.cell[c, pl.ds(R, L - R), :] = jnp.zeros((L - R, 2 * W), bf16)
         w.put_back[...] = one_hot(w.index[C : C + 1, pl.ds(0, s.face_pad)] == iota((s.own, s.face_pad), 0))
         for q in range(s.blocks):
@@ -158,8 +169,8 @@
             if s.face_pad > s.face:
                 w.back[q, pl.ds(s.face, s.face_pad - s.face), :] = jnp.zeros((s.face_pad - s.face, 2 * W), bf16)
 
-    def gather(q):
-        w.part[q] = dot(w.take[:, pl.ds(0, s.own_pad)], w.vec[q, pl.ds(0, s.own_pad), :])
+    def gather():
+        w.part[...] = dot(w.take[:, pl.ds(0, s.own_pad)], w.vec[pl.ds(0, s.own_pad), :])
 
     def middle(step, q):
         last = step == DEGREE - 1
@@ -169,24 +180,26 @@
         for c in range(C):
             rows = pl.ds(c * R, R)
             if step == 0:
-                cell = w.part[q, rows, :] + dot(w.take[rows, pl.ds(s.base, s.depth - s.base)], w.far[q])
+                cell = w.part[rows, span(q)] + dot(w.take[rows, pl.ds(s.base, s.depth - s.base)], w.far[q])
             else:
-                cell = dot(w.take[rows, :], w.vec[q])
+                cell = dot(w.take[rows, :], w.vec[:, span(q)])
             w.cell[c, pl.ds(0, R), :] = cell.astype(bf16)
         for c in range(C):
             wide = dot(w.op_high[c], w.cell[c])
             value = wide[:, :W] + wide[:, W:] + dot(w.op_low[c], w.cell[c, :, pl.ds(0, W)])
-            split_store(w.prod.at[q], c * L, value)
+            split_store(w.prod, c * L, value, q)
         count = s.face if last else 2 * s.face
-        tail = merged(dot(w.put[pl.ds(s.own, count), :], w.prod[q]))
+        tail = merged(dot(w.put[pl.ds(s.own, count), :], w.prod[:, span(q)]))
         w.back_send[step, q] = tail[: s.face]
         back_copy(step, q).start()
         if not last:
             w.edge_send[step, q] = tail[s.face :]
             edge_copy(step, q).start()
 
-    def scatter(q):
-        w.applied[q] = merged(dot(w.put[pl.ds(0, s.own), :], w.prod[q]))
+    def scatter():
+        wide = dot(w.put[pl.ds(0, s.own), :], w.prod[...])
+        for q in blocks:
+            w.applied[q] = merged(wide, q)
 
     def advance(step, applied, current, earlier):
         if step == 0:
@@ -208,7 +221,7 @@
             done(q)
             return
         w.stages[step, :, columns] = following
-        split_store(w.vec.at[q], 0, following)
+        split_store(w.vec, 0, following, q)
         edge_copy(step, q).wait()
 
         def edge(k):
@@ -216,30 +229,24 @@
 
         outer = advance(step, w.back_send[step, q] + w.edge_recv[step, q], edge(step), edge(step - 1) if step else None)
         w.edges[step, q] = outer
-        split_store(w.vec.at[q], s.own, outer)
-
-    blocks = range(s.blocks)
+        split_store(w.vec, s.own, outer, q)
+
     setup_take()
     setup_ops()
     setup_put()
     ready()
     for q in blocks:
         face_copy(q).start()
-    for q in blocks:
-        gather(q)
+    gather()
     for q in blocks:
         middle(0, q)
-    for q in blocks:
-        scatter(q)
+    scatter()
     for step in range(1, DEGREE):
         for q in blocks:
             finish(step - 1, q)
             middle(step, q)
-        if step < DEGREE - 1:
-            for q in blocks:
-                scatter(q)
+        scatter()
     for q in blocks:
-        scatter(q)
         finish(DEGREE - 1, q)
 
 
@@ -297,6 +304,12 @@
         return pltpu.make_async_remote_copy(
             src_ref=w.cross_send, dst_ref=w.cross_recv,
             send_sem=w.cross_ssem, recv_sem=w.cross_rsem,
+            device_id={"band": other}, device_id_type=MESH)
+
+    def norm_copy():
+        return pltpu.make_async_remote_copy(
+            src_ref=w.norm_send, dst_ref=w.norm_recv,
+            send_sem=w.norm_ssem, recv_sem=w.norm_rsem,
             device_id={"band": other}, device_id_type=MESH)
 
     def put_sums(m, value):
@@ -331,16 +344,12 @@
     pair_up(0)
     start_all(scatter_copies(0))
     same = own_total(0)
-    w.full[0, core, chip, pl.ds(0, chunk), :] = same
-    squares = (same * same).reshape(chunk // 8, 8, W).sum(0)
-    w.full[0, core, chip, pl.ds(chunk, 8), :] = squares
+    w.full[0, core, chip] = same
     start_all(gather_copies(0))
 
     for q in range(s.blocks):
         band_copy(s, band_ref, w, 0, other, q).wait_send()
         band_copy(s, band_ref, w, 0, band, q).wait_recv()
-    for q in range(s.blocks):
-        band_copy(s, band_ref, w, 1, band, q).start()
     rows = pl.ds(pl.multiple_of(band * half, 16), half)
     far_high, far_low = halves(w.far_band[rows, :])
     near_high, near_low = w.near_high[rows, :], w.near_low[rows, :]
@@ -357,26 +366,33 @@
              + dot_tn(w.left_high[...], w.right_low[...])
              + dot_tn(w.left_low[...], w.right_high[...]))
     core_copy(1).start()
+    band_copy(s, band_ref, w, 1, band, 0).start()
     pair_up(1)
     start_all(scatter_copies(1))
 
     wait_all(gather_copies(0))
     swap_copy(0).start()
     cross = own_total(1)
-    w.cross_send[pl.ds(0, chunk), :] = cross
-    w.cross_send[pl.ds(chunk, 8), :] = squares
+    w.cross_send[...] = cross
     cross_copy().start()
-    cross_copy().wait()
-    cross = pick(cross, w.cross_recv[pl.ds(0, chunk), :]) + pick(w.cross_recv[pl.ds(0, chunk), :], cross)
-    w.full[1, core, chip, pl.ds(0, chunk), :] = cross
-    w.full[1, core, chip, pl.ds(chunk, 8), :] = (
-        2.0 * (cross * cross).reshape(chunk // 8, 8, W).sum(0) + w.cross_recv[pl.ds(chunk, 8), :])
-    start_all(gather_copies(1))
+    for q in range(1, s.blocks):
+        band_copy(s, band_ref, w, 1, band, q).start()
     swap_copy(0).wait()
-    near_block = w.full[0, :, :, pl.ds(0, chunk), :].reshape(W, W)
+    near_block = w.full[0].reshape(W, W)
+
+    def squares(value):
+        return (value * value).reshape(W // 8, 8, W).sum(0)
+
+    near_squares = squares(near_block)
+    w.norm_send[...] = near_squares
+    norm_copy().start()
     block_high, block_low = halves(near_block)
     w.block_high[0] = block_high
     w.block_low[0] = block_low
+    cross_copy().wait()
+    cross = pick(cross, w.cross_recv[...]) + pick(w.cross_recv[...], cross)
+    w.full[1, core, chip] = cross
+    start_all(gather_copies(1))
     near_high, near_low = w.near_high[pl.ds(0, s.own), :], w.near_low[pl.ds(0, s.own), :]
     near_wide = dot(near_high, w.block_high[0]) + dot(near_high, w.block_low[0])
     w.near_prod[...] = near_wide + dot(near_low, w.block_high[0])
@@ -389,9 +405,10 @@
     wait_all(gather_copies(1))
     swap_copy(1).start()
     swap_copy(1).wait()
-    total = jnp.sum(w.full[:, :, :, pl.ds(chunk, 8), :])
+    norm_copy().wait()
+    far_block = w.full[1].reshape(W, W)
+    total = jnp.sum(near_squares + w.norm_recv[...] + 2.0 * squares(far_block))
     norm = jnp.sqrt(jnp.full((1, W), total, f32) + 1e-06)
-    far_block = w.full[1, :, :, pl.ds(0, chunk), :].reshape(W, W)
     far_block = pick(far_block, jnp.transpose(far_block))
     block_high, block_low = halves(far_block)
     w.block_high[1] = block_high
@@ -412,8 +429,10 @@
         greeted.append({"band": 1 - lax.axis_index("band")})
         for j in range(1, s.chips):
             greeted.append({"dom": lax.rem(chip + j, s.chips) * 2 + core})
-    for device in greeted:
-        pl.semaphore_signal(barrier, inc=1, device_id=device, device_id_type=MESH)
+
+    def greet():
+        for device in greeted:
+            pl.semaphore_signal(barrier, inc=1, device_id=device, device_id_type=MESH)
 
     def ready():
         pl.semaphore_wait(barrier, len(greeted))
@@ -426,10 +445,10 @@
         def send(q):
             band_copy(s, owned, w, 0, 1 - lax.axis_index("band"), q).start()
 
-        filter_steps(s, ready, send, wave_ref, ops_ref, map_ref, face_ref, owned, w)
+        filter_steps(s, greet, ready, send, wave_ref, ops_ref, map_ref, face_ref, owned, w)
         gram_steps(s, owned, out_ref, w)
     else:
-        filter_steps(s, ready, lambda q: None, wave_ref, ops_ref, map_ref, face_ref, out_ref, w)
+        filter_steps(s, greet, ready, lambda q: None, wave_ref, ops_ref, map_ref, face_ref, out_ref, w)
 
 
 def scratch_of(s):
@@ -438,19 +457,22 @@
     scratch = dict(
         index=V((128, max(L, s.face_pad)), f32),
         face_rows=V((s.face, s.own_pad), bf16),
-        vec=V((s.blocks, s.depth, 2 * s.block), bf16),
+        vec=V((s.depth, 2 * W), bf16),
         take=V((C * R, s.depth), bf16),
         put=V((s.own + 2 * s.face, C * L), bf16),
         put_back=V((s.own, s.face_pad), bf16),
         ops=V((s.nodes, C, s.nodes), f32),
-        ops_sem=dma,
+        map=V((C, s.nodes), jnp.int32),
+        face=V((1, s.face), jnp.int32),
+        wave=V((s.own, W), f32),
+        input_sem=dma((4,)),
         op_pad=V((C, R, L), f32),
         op_high=V((C, R, L), bf16),
         op_low=V((C, R, L), bf16),
-        part=V((s.blocks, C * R, 2 * s.block), f32),
+        part=V((C * R, 2 * W), f32),
         applied=V((s.blocks, s.own, s.block), f32),
         cell=V((C, L, 2 * s.block), bf16),
-        prod=V((s.blocks, C * L, 2 * s.block), bf16),
+        prod=V((C * L, 2 * W), bf16),
         far=V((s.blocks, s.depth - s.base, 2 * s.block), bf16),
         back=V((s.blocks, s.face_pad, 2 * s.block), bf16),
         stages=V((DEGREE - 1, s.own, W), f32),
@@ -487,9 +509,13 @@
             core_recv=V((2, W // 2, W), f32),
             pair=V((2, n, chunk, W), f32),
             scat_recv=V((2, n - 1, chunk, W), f32),
-            full=V((2, 2, n, s.packet, W), f32),
-            cross_send=V((s.packet, W), f32),
-            cross_recv=V((s.packet, W), f32),
+            full=V((2, 2, n, chunk, W), f32),
+            cross_send=V((chunk, W), f32),
+            cross_recv=V((chunk, W), f32),
+            norm_send=V((8, W), f32),
+            norm_recv=V((8, W), f32),
+            norm_ssem=dma,
+            norm_rsem=dma,
             cross_ssem=dma,
             cross_rsem=dma,
             band_ssem=dma((2, s.blocks)),
@@ -513,7 +539,7 @@
     latest = pl.pallas_call(
         functools.partial(kernel, s, list(scratch)),
         out_shape=jax.ShapeDtypeStruct(wavefun.shape, f32),
-        in_specs=[pl.BlockSpec(memory_space=space) for space in (pltpu.VMEM, pl.ANY, pltpu.VMEM, pltpu.VMEM)],
+        in_specs=[pl.BlockSpec(memory_space=space) for space in (pl.ANY,) * 4],
         out_specs=pl.BlockSpec(memory_space=pltpu.VMEM),
         scratch_shapes=list(scratch.values()),
         compiler_params=pltpu.CompilerParams(

time: 56.8 us -> 53.6 us (0.944)
  Pallas kernels: 54.5 us -> 51.3 us
    pallas_call x1, Pallas kernels: 54.5 us -> 51.3 us  [on_device(): pl.pallas_call(functools.partial(kernel, s, list(scratch)), out_shape=jax...]
where the time goes in v2:
time: 53.6 us; the launch traced here: 53.4 us
  Pallas kernels  51.3 us (96%)
  local copies, waits for them, and re-layouts  2.14 us (4%)
    pallas_call x1, Pallas kernels, on_device(): pl.pallas_call(functools.partial(kernel, s, list(scratch)), out_shape=jax...  51.3 us
    unnamed x1, local copies, waits for them, and re-layouts  2.14 us

profile of v2, /device:TPU:0, one launch (start us, length us, event | category | flops | bytes accessed | tf_op | source)
XLA Modules:
  0.0 53.4 jit_solution(12964848130948722003)
XLA Ops:
  0.0 51.3 %filtered_bands.1 = f32[864,256]{1,0:T(8,128)} custom-call(f32[864,256]{1,0:T(8,128)} %wave_ref.1, f32[343,4,343]{2,1,0:T(4,128)} %bitcast.2, s32[4,343]{1,0:T(4,128)} %map_ref.1, s32[1,144]{1,0:T(1,128)} %bitcast.3), custom_call_target="tpu_custom_call" | custom-call | tf_op jit(solution)/shard_map/filtered_bands/pallas_call | solution.py:539
  51.3 2.1 %copy.6 = f32[864,256]{1,0:T(8,128)} copy(f32[864,256]{1,0:T(8,128)} %filtered_bands.1) | data formatting | bytes 1769472

commit v3 on v2

--- a/solution.py
+++ b/solution.py
@@ -17,6 +17,7 @@
 f32 = jnp.float32
 bf16 = jnp.bfloat16
 MESH = pl.DeviceIdType.MESH
+VMEM_LIMIT = 58 * 1024 * 1024
 
 
 def round_up(value, step):
@@ -55,6 +56,7 @@
         self.depth = round_up(own + face, 128)
         self.base = own // 128 * 128
         self.half_pad = round_up(own // 2, 128)
+        self.pieces = 3 if own % 48 == 0 else 1
         self.chips = n_dom // 2
         self.chunk = width // n_dom
         self.gram = (
@@ -252,15 +254,20 @@
 
 def band_copy(s, band_ref, w, turn, first, q):
     half = s.own // 2
-    rows = pl.ds(pl.multiple_of(first * half, 8), half)
-    columns = pl.ds(q * s.block, s.block)
+    if turn:
+        size = half // s.pieces
+        rows = pl.ds(pl.multiple_of(first * half + q * size, 8), size)
+        columns = pl.ds(0, s.width)
+    else:
+        rows = pl.ds(pl.multiple_of(first * half, 8), half)
+        columns = pl.ds(q * s.block, s.block)
     return pltpu.make_async_remote_copy(
         src_ref=band_ref.at[rows, columns], dst_ref=w.far_band.at[rows, columns],
         send_sem=w.band_ssem.at[turn, q], recv_sem=w.band_rsem.at[turn, q],
         device_id={"band": 1 - lax.axis_index("band")}, device_id_type=MESH)
 
 
-def gram_steps(s, band_ref, out_ref, w):
+def gram_steps(s, band_ref, wide_ref, total_ref, w):
     me = lax.axis_index("dom")
     band = lax.axis_index("band")
     other = 1 - band
@@ -274,25 +281,34 @@
             send_sem=w.core_ssem.at[m], recv_sem=w.core_rsem.at[m],
             device_id={"dom": partner}, device_id_type=MESH)
 
+    upper = chip * 2 // n
+
+    def farthest(i):
+        falling, rising = n - 1 - i, i
+        falling = falling - (chip - falling + n) // n
+        rising = rising + (rising - chip + n) // n
+        return (1 - upper) * falling + upper * rising
+
+    def spread(i, source, target, send_sem, recv_sem):
+        chip_to = farthest(i)
+        slot = lax.rem(chip_to - chip + n, n) - 1
+        return pltpu.make_async_remote_copy(
+            src_ref=source(chip_to), dst_ref=target(slot),
+            send_sem=send_sem.at[i], recv_sem=recv_sem.at[slot],
+            device_id={"dom": chip_to * 2 + core}, device_id_type=MESH)
+
     def scatter_copies(m):
-        copies = []
-        for j in range(1, n):
-            target = lax.rem(chip + j, n)
-            copies.append(pltpu.make_async_remote_copy(
-                src_ref=w.pair.at[m, target], dst_ref=w.scat_recv.at[m, j - 1],
-                send_sem=w.scat_ssem.at[m, j - 1], recv_sem=w.scat_rsem.at[m, j - 1],
-                device_id={"dom": target * 2 + core}, device_id_type=MESH))
-        return copies
+        return [
+            spread(i, lambda t: w.pair.at[m, t], lambda slot: w.scat_recv.at[m, slot], w.scat_ssem.at[m], w.scat_rsem.at[m])
+            for i in range(n - 1)
+        ]
 
     def gather_copies(m):
-        copies = []
-        for j in range(1, n):
-            target = lax.rem(chip + j, n)
-            copies.append(pltpu.make_async_remote_copy(
-                src_ref=w.full.at[m, core, chip], dst_ref=w.full.at[m, core, chip],
-                send_sem=w.gath_ssem.at[m, j - 1], recv_sem=w.gath_rsem.at[m, j - 1],
-                device_id={"dom": target * 2 + core}, device_id_type=MESH))
-        return copies
+        return [
+            spread(i, lambda t: w.full.at[m, core, chip], lambda slot: w.full.at[m, core, chip],
+                   w.gath_ssem.at[m], w.gath_rsem.at[m])
+            for i in range(n - 1)
+        ]
 
     def swap_copy(m):
         return pltpu.make_async_remote_copy(
@@ -327,7 +343,9 @@
             total = total + w.scat_recv[m, j]
         return total
 
-    high, low = halves(band_ref[...])
+    owned = band_ref.at[pl.ds(0, s.own), :]
+    high, low = halves(owned[...])
+
     def fill(ref, value):
         count, size = value.shape[0], ref.shape[0]
         ref[pl.ds(0, count), :] = value
@@ -336,7 +354,7 @@
 
     fill(w.near_high, high)
     fill(w.near_low, low)
-    turned_high, turned_low = halves(jnp.transpose(w.bands[...]))
+    turned_high, turned_low = halves(jnp.transpose(band_ref[...]))
     put_sums(0, dot(turned_high, w.near_high[...])
              + dot(turned_high, w.near_low[...])
              + dot(turned_low, w.near_high[...]))
@@ -348,8 +366,8 @@
     start_all(gather_copies(0))
 
     for q in range(s.blocks):
-        band_copy(s, band_ref, w, 0, other, q).wait_send()
-        band_copy(s, band_ref, w, 0, band, q).wait_recv()
+        band_copy(s, owned, w, 0, other, q).wait_send()
+        band_copy(s, owned, w, 0, band, q).wait_recv()
     rows = pl.ds(pl.multiple_of(band * half, 16), half)
     far_high, far_low = halves(w.far_band[rows, :])
     near_high, near_low = w.near_high[rows, :], w.near_low[rows, :]
@@ -366,7 +384,8 @@
              + dot_tn(w.left_high[...], w.right_low[...])
              + dot_tn(w.left_low[...], w.right_high[...]))
     core_copy(1).start()
-    band_copy(s, band_ref, w, 1, band, 0).start()
+    for q in range(s.pieces - 1):
+        band_copy(s, owned, w, 1, band, q).start()
     pair_up(1)
     start_all(scatter_copies(1))
 
@@ -375,8 +394,7 @@
     cross = own_total(1)
     w.cross_send[...] = cross
     cross_copy().start()
-    for q in range(1, s.blocks):
-        band_copy(s, band_ref, w, 1, band, q).start()
+    band_copy(s, owned, w, 1, band, s.pieces - 1).start()
     swap_copy(0).wait()
     near_block = w.full[0].reshape(W, W)
 
@@ -396,9 +414,9 @@
     near_high, near_low = w.near_high[pl.ds(0, s.own), :], w.near_low[pl.ds(0, s.own), :]
     near_wide = dot(near_high, w.block_high[0]) + dot(near_high, w.block_low[0])
     w.near_prod[...] = near_wide + dot(near_low, w.block_high[0])
-    for q in range(s.blocks):
-        band_copy(s, band_ref, w, 1, band, q).wait_send()
-        band_copy(s, band_ref, w, 1, other, q).wait_recv()
+    for q in range(s.pieces):
+        band_copy(s, owned, w, 1, band, q).wait_send()
+        band_copy(s, owned, w, 1, other, q).wait_recv()
     high, low = halves(w.far_band[...])
     w.far_high[...] = high
     w.far_low[...] = low
@@ -407,18 +425,30 @@
     swap_copy(1).wait()
     norm_copy().wait()
     far_block = w.full[1].reshape(W, W)
-    total = jnp.sum(near_squares + w.norm_recv[...] + 2.0 * squares(far_block))
-    norm = jnp.sqrt(jnp.full((1, W), total, f32) + 1e-06)
+    total_ref[...] = near_squares + w.norm_recv[...] + 2.0 * squares(far_block)
     far_block = pick(far_block, jnp.transpose(far_block))
     block_high, block_low = halves(far_block)
     w.block_high[1] = block_high
     w.block_low[1] = block_low
     wide = dot(w.far_high[...], w.block_high[1]) + dot(w.far_high[...], w.block_low[1])
-    wide = wide + dot(w.far_low[...], w.block_high[1]) + w.near_prod[...]
-    out_ref[...] = 1.5 * band_ref[...] - wide * (0.5 / norm)
-
-
-def kernel(s, names, wave_ref, ops_ref, map_ref, face_ref, out_ref, *scratch):
+    wide_ref[...] = wide + dot(w.far_low[...], w.block_high[1]) + w.near_prod[...]
+
+
+def settle_kernel(s, wide_ref, band_ref, total_ref, out_ref, stage, sem):
+    norm = jnp.sqrt(jnp.full((1, s.width), jnp.sum(total_ref[...]), f32) + 1e-06)
+    scale = 0.5 / norm
+    size = s.own // 4
+    copies = []
+    for k in range(4):
+        rows = pl.ds(k * size, size)
+        stage[rows, :] = 1.5 * band_ref[rows, :] - wide_ref[rows, :] * scale
+        copies.append(pltpu.make_async_copy(stage.at[rows, :], out_ref.at[rows, :], sem.at[k]))
+        copies[k].start()
+    wait_all(copies)
+
+
+def kernel(s, names, wave_ref, ops_ref, map_ref, face_ref, *refs):
+    outs, scratch = refs[: len(refs) - len(names)], refs[len(refs) - len(names) :]
     w = types.SimpleNamespace(**dict(zip(names, scratch)))
     me = lax.axis_index("dom")
     barrier = pltpu.get_barrier_semaphore()
@@ -438,17 +468,18 @@
         pl.semaphore_wait(barrier, len(greeted))
 
     if s.gram:
+        wide_ref, band_ref, total_ref = outs
         if s.own_pad > s.own:
-            w.bands[pl.ds(s.own, s.own_pad - s.own), :] = jnp.zeros((s.own_pad - s.own, s.width), f32)
-        owned = w.bands.at[pl.ds(0, s.own), :]
+            band_ref[pl.ds(s.own, s.own_pad - s.own), :] = jnp.zeros((s.own_pad - s.own, s.width), f32)
+        owned = band_ref.at[pl.ds(0, s.own), :]
 
         def send(q):
             band_copy(s, owned, w, 0, 1 - lax.axis_index("band"), q).start()
 
         filter_steps(s, greet, ready, send, wave_ref, ops_ref, map_ref, face_ref, owned, w)
-        gram_steps(s, owned, out_ref, w)
+        gram_steps(s, band_ref, wide_ref, total_ref, w)
     else:
-        filter_steps(s, greet, ready, lambda q: None, wave_ref, ops_ref, map_ref, face_ref, out_ref, w)
+        filter_steps(s, greet, ready, lambda q: None, wave_ref, ops_ref, map_ref, face_ref, outs[0], w)
 
 
 def scratch_of(s):
@@ -492,7 +523,6 @@
     )
     if s.gram:
         scratch |= dict(
-            bands=V((s.own_pad, W), f32),
             far_band=V((s.own, W), f32),
             near_high=V((s.own_pad, W), bf16),
             near_low=V((s.own_pad, W), bf16),
@@ -518,8 +548,8 @@
             norm_rsem=dma,
             cross_ssem=dma,
             cross_rsem=dma,
-            band_ssem=dma((2, s.blocks)),
-            band_rsem=dma((2, s.blocks)),
+            band_ssem=dma((2, max(s.blocks, s.pieces))),
+            band_rsem=dma((2, max(s.blocks, s.pieces))),
             core_ssem=dma((2,)),
             core_rsem=dma((2,)),
             swap_ssem=dma((2,)),
@@ -536,18 +566,31 @@
     s = Sizes(lax.axis_size("dom"), lax.axis_size("band"), wavefun.shape[0], wavefun.shape[1],
               cell_map.shape[0], cell_map.shape[1], face_list.shape[0])
     scratch = scratch_of(s)
-    latest = pl.pallas_call(
+    shapes = [wavefun.shape]
+    if s.gram:
+        shapes += [(s.own_pad, s.width), (8, s.width)]
+    inside = pl.BlockSpec(memory_space=pltpu.VMEM)
+    outs = pl.pallas_call(
         functools.partial(kernel, s, list(scratch)),
-        out_shape=jax.ShapeDtypeStruct(wavefun.shape, f32),
-        in_specs=[pl.BlockSpec(memory_space=space) for space in (pl.ANY,) * 4],
-        out_specs=pl.BlockSpec(memory_space=pltpu.VMEM),
+        out_shape=[pltpu.VMEM(shape, f32) if s.gram else jax.ShapeDtypeStruct(shape, f32) for shape in shapes],
+        in_specs=[pl.BlockSpec(memory_space=pl.ANY)] * 4,
+        out_specs=[inside] * len(shapes),
         scratch_shapes=list(scratch.values()),
         compiler_params=pltpu.CompilerParams(
-            collective_id=0, has_side_effects=True, vmem_limit_bytes=60 * 1024 * 1024),
+            collective_id=0, has_side_effects=True, vmem_limit_bytes=VMEM_LIMIT),
         name="filtered_bands",
     )(wavefun, jnp.swapaxes(cell_ops, 0, 1), cell_map, face_list.reshape(1, -1))
     if s.gram:
-        return latest
+        return pl.pallas_call(
+            functools.partial(settle_kernel, s),
+            out_shape=jax.ShapeDtypeStruct(wavefun.shape, f32),
+            in_specs=[inside] * 3,
+            out_specs=pl.BlockSpec(memory_space=pl.ANY),
+            scratch_shapes=[pltpu.VMEM(wavefun.shape, f32), pltpu.SemaphoreType.DMA((4,))],
+            compiler_params=pltpu.CompilerParams(vmem_limit_bytes=8 * 1024 * 1024),
+            name="settled_bands",
+        )(*outs)
+    latest = outs[0]
     full_bands = lax.all_gather(latest, "band", axis=1, tiled=True)
     partial_value = jnp.einsum("nb,nc->bc", full_bands, full_bands, precision=lax.Precision.HIGHEST)
     margin = lax.psum(partial_value, "dom")

time: 53.6 us -> 51.3 us (0.957)
  local copies, waits for them, and re-layouts: 2.14 us -> 0 us
    unnamed x1 -> x0, local copies, waits for them, and re-layouts: 2.14 us -> none
    pallas_call x1 -> x2, Pallas kernels: 51.3 us -> 50.9 us  [the longest x1 49.8 us: on_device(): pl.pallas_call(functools.partial(kernel, s, list(scratch)), out_shape=[pl...]
where the time goes in v3:
time: 51.3 us; the launch traced here: 51.1 us
  Pallas kernels  50.9 us (99%)
    pallas_call x1, Pallas kernels, on_device(): pl.pallas_call(functools.partial(kernel, s, list(scratch)), out_shape=[pl...  49.8 us
    pallas_call x1, Pallas kernels, on_device(): pl.pallas_call(functools.partial(settle_kernel, s), out_shape=jax.ShapeDt...  1.11 us

profile of v3, /device:TPU:0, one launch (start us, length us, event | category | flops | bytes accessed | tf_op | source)
XLA Modules:
  0.0 51.1 jit_solution(11233477498306137339)
XLA Ops:
  0.0 49.8 %filtered_bands.1 = (f32[864,256]{1,0:T(8,128)S(1)}, f32[896,256]{1,0:T(8,128)S(1)}, f32[8,256]{1,0:T(8,128)S(1)}) custom-call(f32[864,256]{1,0:T(8,128)} %wave_ref.1, f32[343,4,343]{2,1,0:T(4,128)} %bitcast.2, s32[4,343]{1,0:T(4,128)} %map_ref.1, s32[1,144]{1,0:T(1,128)} %bitcast.3), custom_call_target="tpu_custom_call" | custom-call | tf_op jit(solution)/shard_map/filtered_bands/pallas_call | solution.py:573
  49.8 1.1 %settled_bands.1 = f32[864,256]{1,0:T(8,128)} custom-call(f32[864,256]{1,0:T(8,128)S(1)} %get-tuple-element.8.wide_ref, f32[896,256]{1,0:T(8,128)S(1)} %get-tuple-element.9.band_ref, f32[8,256]{1,0:T(8,128)S(1)} %get-tuple-element.10.total_ref), custom_call_target="tpu_custom_call" | custom-call | tf_op jit(solution)/shard_map/settled_bands/pallas_call | solution.py:584

commit v4 on v3

--- a/solution.py
+++ b/solution.py
@@ -56,7 +56,7 @@
         self.depth = round_up(own + face, 128)
         self.base = own // 128 * 128
         self.half_pad = round_up(own // 2, 128)
-        self.pieces = 3 if own % 48 == 0 else 1
+        self.pieces = 2
         self.chips = n_dom // 2
         self.chunk = width // n_dom
         self.gram = (
@@ -233,12 +233,21 @@
         w.edges[step, q] = outer
         split_store(w.vec, s.own, outer, q)
 
+    quarter = me * 4 // s.n_dom
+
+    def begin_where(condition):
+        @pl.when(condition)
+        def _():
+            ready()
+            for q in blocks:
+                face_copy(q).start()
+
     setup_take()
+    begin_where(quarter >= 2)
     setup_ops()
+    begin_where(quarter == 1)
     setup_put()
-    ready()
-    for q in blocks:
-        face_copy(q).start()
+    begin_where(quarter == 0)
     gather()
     for q in blocks:
         middle(0, q)
@@ -252,19 +261,26 @@
         finish(DEGREE - 1, q)
 
 
-def band_copy(s, band_ref, w, turn, first, q):
-    half = s.own // 2
-    if turn:
-        size = half // s.pieces
-        rows = pl.ds(pl.multiple_of(first * half + q * size, 8), size)
-        columns = pl.ds(0, s.width)
-    else:
-        rows = pl.ds(pl.multiple_of(first * half, 8), half)
-        columns = pl.ds(q * s.block, s.block)
+def half_rows(s, which):
+    return pl.ds(pl.multiple_of(which * (s.own // 2), 16), s.own // 2)
+
+
+def remote_band(source, target, w, turn, q):
     return pltpu.make_async_remote_copy(
-        src_ref=band_ref.at[rows, columns], dst_ref=w.far_band.at[rows, columns],
+        src_ref=source, dst_ref=target,
         send_sem=w.band_ssem.at[turn, q], recv_sem=w.band_rsem.at[turn, q],
         device_id={"band": 1 - lax.axis_index("band")}, device_id_type=MESH)
+
+
+def block_copy(w, q):
+    return remote_band(w.block_send.at[q], w.block_recv.at[q], w, 0, q)
+
+
+def piece_copy(s, band_ref, w, q):
+    half = s.own // 2
+    size = half // s.pieces
+    first = lax.axis_index("band") * half + q * size
+    return remote_band(band_ref.at[pl.ds(pl.multiple_of(first, 8), size), :], w.far_band.at[pl.ds(q * size, size), :], w, 1, q)
 
 
 def gram_steps(s, band_ref, wide_ref, total_ref, w):
@@ -366,10 +382,11 @@
     start_all(gather_copies(0))
 
     for q in range(s.blocks):
-        band_copy(s, owned, w, 0, other, q).wait_send()
-        band_copy(s, owned, w, 0, band, q).wait_recv()
-    rows = pl.ds(pl.multiple_of(band * half, 16), half)
-    far_high, far_low = halves(w.far_band[rows, :])
+        block_copy(w, q).wait()
+    rows = half_rows(s, band)
+    far_high, far_low = halves(jnp.concatenate([w.block_recv[q] for q in range(s.blocks)], axis=1))
+    w.far_high[rows, :] = far_high
+    w.far_low[rows, :] = far_low
     near_high, near_low = w.near_high[rows, :], w.near_low[rows, :]
     first = band == 0
 
@@ -385,7 +402,7 @@
              + dot_tn(w.left_low[...], w.right_high[...]))
     core_copy(1).start()
     for q in range(s.pieces - 1):
-        band_copy(s, owned, w, 1, band, q).start()
+        piece_copy(s, owned, w, q).start()
     pair_up(1)
     start_all(scatter_copies(1))
 
@@ -394,7 +411,7 @@
     cross = own_total(1)
     w.cross_send[...] = cross
     cross_copy().start()
-    band_copy(s, owned, w, 1, band, s.pieces - 1).start()
+    piece_copy(s, owned, w, s.pieces - 1).start()
     swap_copy(0).wait()
     near_block = w.full[0].reshape(W, W)
 
@@ -415,11 +432,11 @@
     near_wide = dot(near_high, w.block_high[0]) + dot(near_high, w.block_low[0])
     w.near_prod[...] = near_wide + dot(near_low, w.block_high[0])
     for q in range(s.pieces):
-        band_copy(s, owned, w, 1, band, q).wait_send()
-        band_copy(s, owned, w, 1, other, q).wait_recv()
+        piece_copy(s, owned, w, q).wait()
+    rows = half_rows(s, other)
     high, low = halves(w.far_band[...])
-    w.far_high[...] = high
-    w.far_low[...] = low
+    w.far_high[rows, :] = high
+    w.far_low[rows, :] = low
     wait_all(gather_copies(1))
     swap_copy(1).start()
     swap_copy(1).wait()
@@ -474,7 +491,9 @@
         owned = band_ref.at[pl.ds(0, s.own), :]
 
         def send(q):
-            band_copy(s, owned, w, 0, 1 - lax.axis_index("band"), q).start()
+            rows = half_rows(s, 1 - lax.axis_index("band"))
+            w.block_send[q] = owned[rows, pl.ds(q * s.block, s.block)]
+            block_copy(w, q).start()
 
         filter_steps(s, greet, ready, send, wave_ref, ops_ref, map_ref, face_ref, owned, w)
         gram_steps(s, band_ref, wide_ref, total_ref, w)
@@ -523,7 +542,9 @@
     )
     if s.gram:
         scratch |= dict(
-            far_band=V((s.own, W), f32),
+            far_band=V((s.own // 2, W), f32),
+            block_send=V((s.blocks, s.own // 2, s.block), f32),
+            block_recv=V((s.blocks, s.own // 2, s.block), f32),
             near_high=V((s.own_pad, W), bf16),
             near_low=V((s.own_pad, W), bf16),
             left_high=V((s.half_pad, W), bf16),

time: 51.3 us -> 50.4 us (0.982)
  Pallas kernels: 50.9 us -> 50.1 us
    pallas_call x1, Pallas kernels: 49.8 us -> 49 us  [on_device(): pl.pallas_call(functools.partial(kernel, s, list(scratch)), out_shape=[pl...]
where the time goes in v4:
time: 50.4 us; the launch traced here: 50.2 us
  Pallas kernels  50.1 us (99%)
    pallas_call x1, Pallas kernels, on_device(): pl.pallas_call(functools.partial(kernel, s, list(scratch)), out_shape=[pl...  49 us
    pallas_call x1, Pallas kernels, on_device(): pl.pallas_call(functools.partial(settle_kernel, s), out_shape=jax.ShapeDt...  1.11 us

profile of v4, /device:TPU:0, one launch (start us, length us, event | category | flops | bytes accessed | tf_op | source)
XLA Modules:
  0.0 50.2 jit_solution(4132266429263002458)
XLA Ops:
  0.0 49.0 %filtered_bands.1 = (f32[864,256]{1,0:T(8,128)S(1)}, f32[896,256]{1,0:T(8,128)S(1)}, f32[8,256]{1,0:T(8,128)S(1)}) custom-call(f32[864,256]{1,0:T(8,128)} %wave_ref.1, f32[343,4,343]{2,1,0:T(4,128)} %bitcast.2, s32[4,343]{1,0:T(4,128)} %map_ref.1, s32[1,144]{1,0:T(1,128)} %bitcast.3), custom_call_target="tpu_custom_call" | custom-call | tf_op jit(solution)/shard_map/filtered_bands/pallas_call | solution.py:594
  49.0 1.1 %settled_bands.1 = f32[864,256]{1,0:T(8,128)} custom-call(f32[864,256]{1,0:T(8,128)S(1)} %get-tuple-element.8.wide_ref, f32[896,256]{1,0:T(8,128)S(1)} %get-tuple-element.9.band_ref, f32[8,256]{1,0:T(8,128)S(1)} %get-tuple-element.10.total_ref), custom_call_target="tpu_custom_call" | custom-call | tf_op jit(solution)/shard_map/settled_bands/pallas_call | solution.py:605
